TPU v7x, 256 devices: a whole 4x4x8 slice. The times are simulated.
256 devices in a mesh: row: 16 (over z_lo, x, core), col: 4 (over y), item: 4 (over z_hi).
Axes of the slice: x: 4, y: 4, z: 8 (z_hi: 4, z_lo: 2; z = z_hi * 2 + z_lo), core: 2. Of those that a mesh axis runs over, the one named last changes fastest.
Arguments:
- tokens: bfloat16 [4, 16, 64, 2432], P('item', 'row', 'col'), may hold values from -6 to 6
- text_keys_values: bfloat16 [4, 154, 2, 2048], P('item', None, None, 'row'), may hold values from -200 to 200
- text_length: int32 [4], P('item'), may hold values from 2 to 154, as said below
- modulation: float32 [4, 8, 2432], P('item'), may hold values from -4 to 4
- input_weight: bfloat16 [2432, 3, 2048], P(None, None, 'row'), may hold values from -0.125 to 0.125
- norm_gain: float32 [2, 64], replicated, may hold values from 1 to 3
- output_weight: bfloat16 [2048, 2432], P('row'), may hold values from -0.125 to 0.125
- up_weight: bfloat16 [2432, 9728], P(None, 'row'), may hold values from -0.125 to 0.125
- down_weight: bfloat16 [9728, 2432], P('row'), may hold values from -0.0625 to 0.0625
- final_weight: bfloat16 [2432, 64], replicated, may hold values from -0.125 to 0.125
- step_index: int32 [1], replicated, may hold values from 0 to 27
- latent: float32 [4, 16, 4096], P('item', 'row', 'col'), may hold values from -6 to 6
Outputs:
- tokens_out: bfloat16 [4, 16, 64, 2432], P('item', 'row', 'col')
- velocity: float32 [4, 16, 4096], P('item', 'row', 'col')
- latent_next: float32 [4, 16, 4096], P('item', 'row', 'col')
Inputs may be any that keep to these rules, and one draw needn't show every extreme that they name: `text_length`: at least one sequence has all 154 text tokens valid.
All inputs are finite; a program needn't handle non-finite values.
Results may differ from a plain program's by a relative error of at most 0.024.
Values may be sent and summed in bfloat16 or wider, within the bound.
A program may use at most 64 MiB of HBM per device.

v0:
```python
import jax
import jax.numpy as jnp
from jax import lax
from jax.sharding import PartitionSpec as P

HD = 64
STEPS = 28
EPSILON = 1e-06
SHIFT_FACTOR = 3.0
GUIDANCE = 4.5
MASKED = -1e30


def partner_2(value, axis, apart):
    mask = 2**apart
    pairs = [(source, source ^ mask) for source in range(lax.axis_size(axis))]
    return lax.ppermute(value, axis, pairs)


def layer_norm(values):
    center = values - jnp.mean(values, axis=-1, keepdims=True)
    spread = jnp.mean(center * center, axis=-1, keepdims=True)
    return center * lax.rsqrt(spread + EPSILON)


def modulate(values, shift_term, scale_term):
    return (layer_norm(values) * (1.0 + scale_term) + shift_term).astype(jnp.bfloat16)


def root_norm(values, gain_row):
    return (
        values * lax.rsqrt(jnp.mean(values * values, axis=-1, keepdims=True) + EPSILON) * gain_row
    )


def noise_level(position):
    linear = 1.0 - position / STEPS
    return SHIFT_FACTOR * linear / (1.0 + (SHIFT_FACTOR - 1.0) * linear)


def on_device(
    tokens,
    text_keys_values,
    text_length,
    modulation,
    input_weight,
    norm_gain,
    output_weight,
    up_weight,
    down_weight,
    final_weight,
    step_index,
    latent,
):
    tile_rows = tokens.shape[1] * tokens.shape[2]
    model_width = tokens.shape[3]
    mod_rows = modulation[0]
    row_position = lax.axis_index("row")
    stripe_tokens = lax.all_gather(tokens, "row", axis=1, tiled=True)
    stripe_states = stripe_tokens.reshape(-1, model_width).astype(jnp.float32)
    stripe_rows = stripe_states.shape[0]
    local_width = input_weight.shape[2]
    local_heads = local_width // HD
    attn_input = modulate(stripe_states, mod_rows[0], mod_rows[1])
    projected = jnp.dot(
        attn_input,
        input_weight.reshape(model_width, 3 * local_width),
        preferred_element_type=jnp.float32,
    )
    projected = projected.reshape(stripe_rows, 3, local_heads, HD)
    queries = root_norm(projected[:, 0], norm_gain[0]).astype(jnp.bfloat16).transpose(1, 0, 2)
    keys_image = (
        root_norm(projected[:, 1], norm_gain[1])
        .astype(jnp.bfloat16)
        .reshape(stripe_rows, local_width)
    )
    values_image = projected[:, 2].astype(jnp.bfloat16).reshape(stripe_rows, local_width)
    text_pairs = text_keys_values[0]
    keys_text = text_pairs[:, 0].reshape(-1, local_heads, HD)
    values_text = text_pairs[:, 1].reshape(-1, local_heads, HD)
    text_valid = jnp.arange(keys_text.shape[0]) < text_length[0]
    text_scores = jnp.einsum(
        "hsd,thd->hst", queries, keys_text, preferred_element_type=jnp.float32
    ) * HD ** (-0.5)
    text_scores = jnp.where(text_valid[None, None, :], text_scores, MASKED)
    largest = jnp.max(text_scores, axis=-1)
    text_weights = jnp.exp(text_scores - largest[..., None])
    total_mass = jnp.sum(text_weights, axis=-1)
    weighted = jnp.einsum(
        "hst,thd->hsd",
        text_weights.astype(jnp.bfloat16),
        values_text,
        preferred_element_type=jnp.float32,
    )

    def one_block(running, block_pair):
        running_max, running_mass, running_sum = running
        key_block, value_block = block_pair
        scores = jnp.einsum(
            "hsd,khd->hsk", queries, key_block, preferred_element_type=jnp.float32
        ) * HD ** (-0.5)
        new_max = jnp.maximum(running_max, jnp.max(scores, axis=-1))
        factor = jnp.exp(running_max - new_max)
        weights = jnp.exp(scores - new_max[..., None])
        new_mass = running_mass * factor + jnp.sum(weights, axis=-1)
        new_sum = running_sum * factor[..., None] + jnp.einsum(
            "hsk,khd->hsd",
            weights.astype(jnp.bfloat16),
            value_block,
            preferred_element_type=jnp.float32,
        )
        return ((new_max, new_mass, new_sum), None)

    key_piece = lax.all_gather(keys_image, "col", axis=0, tiled=True)
    value_piece = lax.all_gather(values_image, "col", axis=0, tiled=True)
    blocks = key_piece.shape[0] // stripe_rows
    key_blocks = key_piece.reshape(blocks, stripe_rows, local_heads, HD)
    value_blocks = value_piece.reshape(blocks, stripe_rows, local_heads, HD)
    result, unused = lax.scan(
        one_block, (largest, total_mass, weighted), (key_blocks, value_blocks)
    )
    largest, total_mass, weighted = result
    attended = (
        (weighted / total_mass[..., None])
        .astype(jnp.bfloat16)
        .transpose(1, 0, 2)
        .reshape(stripe_rows, local_width)
    )
    attention = lax.psum(
        jnp.dot(attended, output_weight, preferred_element_type=jnp.float32).astype(jnp.bfloat16),
        "row",
    ).astype(jnp.float32)
    stripe_middle = stripe_states + mod_rows[2] * attention
    feed_input = modulate(stripe_middle, mod_rows[3], mod_rows[4])
    hidden = jax.nn.gelu(
        jnp.dot(feed_input, up_weight, preferred_element_type=jnp.float32), approximate=True
    ).astype(jnp.bfloat16)
    middle = lax.dynamic_slice_in_dim(stripe_middle, row_position * tile_rows, tile_rows, 0)
    feed = lax.psum_scatter(
        jnp.dot(hidden, down_weight, preferred_element_type=jnp.float32).astype(jnp.bfloat16),
        "row",
        scatter_dimension=0,
        tiled=True,
    ).astype(jnp.float32)
    leaving = middle + mod_rows[5] * feed
    tokens_out = leaving.astype(jnp.bfloat16).reshape(tokens.shape)
    final_input = modulate(leaving, mod_rows[6], mod_rows[7])
    raw_velocity = jnp.dot(final_input, final_weight, preferred_element_type=jnp.float32).reshape(
        1, tokens.shape[1], -1
    )
    partner = partner_2(raw_velocity, "item", 0)
    is_guided = lax.axis_index("item") % 2 == 0
    guided = jnp.where(is_guided, raw_velocity, partner)
    unguided = jnp.where(is_guided, partner, raw_velocity)
    velocity = unguided + GUIDANCE * (guided - unguided)
    position = step_index[0].astype(jnp.float32)
    step_size = noise_level(position + 1.0) - noise_level(position)
    return (tokens_out, velocity, latent + step_size * velocity)


def solution(mesh):
    in_specs = (
        P("item", "row", "col", None),
        P("item", None, None, "row"),
        P("item"),
        P("item", None, None),
        P(None, None, "row"),
        P(),
        P("row", None),
        P(None, "row"),
        P("row", None),
        P(),
        P(),
        P("item", "row", "col"),
    )
    out_specs = (P("item", "row", "col", None), P("item", "row", "col"), P("item", "row", "col"))
    return jax.shard_map(
        on_device, mesh=mesh, in_specs=in_specs, out_specs=out_specs, check_vma=False
    )
```

profile of v0, /device:TPU:8, one launch (start us, length us, event | category | flops | bytes accessed | tf_op | source)
XLA Modules:
  0.0 311.7 jit_solution(12788335768457517483)
XLA Ops:
  8.0 4.1 %copy.26 = bf16[2432,3,128]{0,2,1:T(8,128)(2,1)} copy(bf16[2432,3,128]{2,0,1:T(8,128)(2,1)} %param.18) | data formatting | bytes 3735552 | tf_op args[4]
  13.9 34.3 %all-gather.2.cloned.1.call-done = bf16[1,16,16,2432]{3,2,0,1:T(8,128)(2,1)} async-done(((bf16[1,1,16,2432]{3,2,0,1:T(8,128)(2,1)}), bf16[1,16,16,2432]{3,2,0,1:T(8,128)(2,1)}) %all-gather.2.cloned.1.call-update) | async-done | bytes 1245200 | tf_op jit(solution)/shard_map/all_gather | solution.py:59
  48.2 1.7 convert_reduce_fusion
  49.9 1.7 multiply_reduce_fusion.1
  53.8 12.6 %all_gather.10 = bf16[1024,128]{0,1:T(8,128)(2,1)S(1)} all-gather(bf16[256,128]{0,1:T(8,128)(2,1)S(1)} %fusion.35), channel_id=1, replica_groups=mesh['row'=16,'col'=4,'item'=4] {'col'}, dimensions={0}, use_global_device_ids=true | all-gather | bytes 327680 | tf_op jit(solution)/shard_map/all_gather | solution.py:114
  68.3 13.0 %all_gather.11 = bf16[1024,128]{0,1:T(8,128)(2,1)} all-gather(bf16[256,128]{0,1:T(8,128)(2,1)S(1)} %bitcast.82), channel_id=1, replica_groups=mesh['row'=16,'col'=4,'item'=4] {'col'}, dimensions={0}, use_global_device_ids=true | all-gather | bytes 327680 | tf_op jit(solution)/shard_map/all_gather | solution.py:115
  81.3 1.8 reshape.191
  83.1 1.7 copy.30
  84.8 6.1 %while.14 = (s32[]{:T(128)}, f32[2,256]{1,0:T(2,128)S(1)}, f32[2,256]{1,0:T(2,128)S(1)}, f32[2,256,64]{1,2,0:T(8,128)S(1)}, bf16[4,256,2,64]{1,3,2,0:T(8,128)(2,...) while((s32[]{:T(128)}, f32[2,256]{1,0:T(2,128)S(1)}, ...), condition=%wide.region_9.10_spmd, body=%wide.region_6.9_spmd.sunk | while | flops 34407424 | bytes 2064985 | solution.py:119
  85.2 1.1 convolution_add_fusion.2
  86.8 1.1 convolution_add_fusion.2
  88.3 1.1 convolution_add_fusion.2
  89.8 1.1 convolution_add_fusion.2
  91.0 2.7 convolution_convert_fusion
  93.7 124.3 %all-reduce.2.cloned.1.call-done = bf16[256,2432]{1,0:T(8,128)(2,1)} async-done(((bf16[256,2432]{1,0:T(8,128)(2,1)}), bf16[256,2432]{1,0:T(8,128)(2,1)}) %all-reduce.2.cloned.1.call-update) | async-done | bytes 1245200 | tf_op jit(solution)/shard_map/psum | solution.py:129
  218.0 2.2 fusion.51
  220.2 1.4 copy-done.2
  222.0 7.5 %convolution_convert_fusion.1 = bf16[256,2432]{1,0:T(8,128)(2,1)} fusion(bf16[608,2432]{1,0:T(8,128)(2,1)S(1)} %copy-done, bf16[2432,608]{0,1:T(8,128)(2,1)} %param.21, f32[256,2432]{1,0:T(8,128)} %copy-done.2, f32[2432]{0:T(1024)S(1)} %get-tuple-element.58, f32[2432]{0:T(1024)S(1)} %copy-done.7, f32[256]{0:T(256)S(1)} %add_rsqrt_fusion.3, ...), kind=kOutput, calls=%fused_computation.16 | convolution fusion | flops 1519280128 | bytes 9671680 | tf_op jit(solution)/shard_map/dot_general | solution.py:140
  229.6 66.3 %reduce-scatter.2.cloned.1.call-done = bf16[16,2432]{1,0:T(8,128)(2,1)} async-done(((bf16[256,2432]{1,0:T(8,128)(2,1)}), bf16[16,2432]{1,0:T(8,128)(2,1)}) %reduce-scatter.2.cloned.1.call-update) | async-done | bytes 77840 | tf_op jit(solution)/shard_map/reduce_scatter | solution.py:139
  295.9 1.1 fusion.49
  297.0 1.7 multiply_reduce_fusion.2
  298.7 1.2 fusion.36
  300.0 2.6 collective-permute-start
  303.3 1.2 collective-permute-done
  (77 shorter events, 8.7 us)
Async XLA Ops:
  7.2 214.8 %copy-start = (bf16[608,2432]{1,0:T(8,128)(2,1)S(1)}, bf16[608,2432]{1,0:T(8,128)(2,1)}, u32[]{:S(2)}) copy-start(bf16[608,2432]{1,0:T(8,128)(2,1)} %param.22) | copy-start | bytes 8871940
  7.2 4.9 %copy-start.4 = (bf16[1,154,2,128]{3,2,1,0:T(2,128)(2,1)S(1)}, bf16[1,154,2,128]{3,2,1,0:T(2,128)(2,1)}, u32[]{:S(2)}) copy-start(bf16[1,154,2,128]{3,2,1,0:T(2,128)(2,1)} %param.15) | copy-start | bytes 236548
  7.2 5.9 %copy-start.9 = (f32[2,64]{1,0:T(2,128)S(1)}, f32[2,64]{1,0:T(2,128)}, u32[]{:S(2)}) copy-start(f32[2,64]{1,0:T(2,128)} %param.19) | copy-start | bytes 1540
  7.2 6.0 %copy-start.6 = (f32[1,8,2432]{2,1,0:T(8,128)S(1)}, f32[1,8,2432]{2,1,0:T(8,128)}, u32[]{:S(2)}) copy-start(f32[1,8,2432]{2,1,0:T(8,128)} %param.17) | copy-start | bytes 233476
  7.2 41.0 %all-gather.2.cloned.1.call-start = ((), (), s32[]{:S(2)}) async-start(), calls=%async_computation.1 | async-start | bytes 1323008 | tf_op jit(solution)/shard_map/all_gather | solution.py:59
  7.9 210.0 %all-reduce.2.cloned.1.call-start = ((), (), s32[]{:S(2)}) async-start(), calls=%async_computation.2 | async-start | bytes 2490368 | tf_op jit(solution)/shard_map/psum | solution.py:129
  48.2 3.5 %copy-start.1 = (bf16[1,16,16,2432]{3,2,0,1:T(8,128)(2,1)S(1)}, bf16[1,16,16,2432]{3,2,0,1:T(8,128)(2,1)}, u32[]{:S(2)}) copy-start(bf16[1,16,16,2432]{3,2,0,1:T(8,128)(2,1)} %all-gather.2.cloned.1.call-done) | copy-start | bytes 3735556
  48.2 4.1 %copy-start.3 = (bf16[2432,3,128]{0,2,1:T(8,128)(2,1)S(1)}, bf16[2432,3,128]{0,2,1:T(8,128)(2,1)}, u32[]{:S(2)}) copy-start(bf16[2432,3,128]{0,2,1:T(8,128)(2,1)} %copy.26) | copy-start | bytes 5603332
  93.6 202.3 %reduce-scatter.2.cloned.1.call-start = ((), (), s32[]{:S(2)}) async-start(), calls=%async_computation.3 | async-start | bytes 1323008 | tf_op jit(solution)/shard_map/reduce_scatter | solution.py:139
  220.1 1.4 copy-start.2
  220.2 1.9 copy-start.7
  222.0 76.7 %copy-start.5 = (bf16[2432,64]{0,1:T(8,128)(2,1)S(1)}, bf16[2432,64]{0,1:T(8,128)(2,1)}, u32[]{:S(2)}) copy-start(bf16[2432,64]{0,1:T(8,128)(2,1)} %param.23) | copy-start | bytes 933892
  229.5 75.0 %copy-start.8 = (f32[1,1,1024]{2,1,0:T(1,128)S(1)}, f32[1,1,1024]{2,1,0:T(1,128)}, u32[]{:S(2)}) copy-start(f32[1,1,1024]{2,1,0:T(1,128)} %param.25) | copy-start | bytes 12292
  300.0 4.5 %collective-permute-start = (f32[1,1,1024]{2,1,0:T(1,128)S(1)}, f32[1,1,1024]{2,1,0:T(1,128)S(1)}, u32[]{:S(2)}, u32[]{:S(2)}) collective-permute-start(f32[1,1,1024]{2,1,0:T(1,128)S(1)} %reshape.194), channel_id=1, source_target_pairs={{0,1},{1,0},{2,3},{3,2},{4,5},{5,4},{6,7},{7,6},{8,9},{9,8},{10,11... | collective-permute-start | bytes 12296 | tf_op jit(solution)/shard_map/ppermute | solution.py:17
Sparse Core Ops, SparseCore 0:
  9.9 38.2 all-gather.1
  93.8 124.1 all-reduce.1
  229.7 66.1 reduce-scatter.1
where the time goes:
time: 312 us
  waiting for transfers between devices  227 us (73%)
  blocking collectives  25.6 us (8%)
  matrix products  18 us (6%)
  between operations  15.4 us (5%)
  local copies, waits for them, and re-layouts  11.5 us (4%)
  other arithmetic  11.5 us (4%)
    psum x1, waiting for transfers between devices, on_device(): lax.psum(jnp.dot(attended, output_weight, preferred_element_type=jnp.floa...  124 us
    reduce_scatter x1, waiting for transfers between devices, on_device(): lax.psum_scatter(jnp.dot(hidden, down_weight, preferred_element_type=jnp....  66.3 us
    all_gather x1, waiting for transfers between devices, on_device(): stripe_tokens = lax.all_gather(tokens, 'row', axis=1, tiled=True)  34.3 us
    all_gather x1, blocking collectives, on_device(): value_piece = lax.all_gather(values_image, 'col', axis=0, tiled=True)  13 us
    all_gather x1, blocking collectives, on_device(): key_piece = lax.all_gather(keys_image, 'col', axis=0, tiled=True)  12.6 us
    dot_general x1, matrix products, on_device(): jnp.dot(hidden, down_weight, preferred_element_type=jnp.float32)  7.51 us
  transfers between devices with their start and end apart: 4, of which 4 were waited for; matrix products, arithmetic and copies ran while one was open for 2% of the time, Pallas kernels for 0%

commit v1 on v0

--- a/solution.py
+++ b/solution.py
@@ -112,7 +112,12 @@
         return ((new_max, new_mass, new_sum), None)
 
     key_piece = lax.all_gather(keys_image, "col", axis=0, tiled=True)
-    value_piece = lax.all_gather(values_image, "col", axis=0, tiled=True)
+    ring = [values_image]
+    for hop in range(3):
+        ring.append(lax.ppermute(ring[-1], "col", [(dev, (dev + 1) % 4) for dev in range(4)]))
+    value_piece = jnp.roll(
+        jnp.concatenate(ring[::-1], axis=0), (lax.axis_index("col") + 1) * ring[0].shape[0], axis=0
+    )
     blocks = key_piece.shape[0] // stripe_rows
     key_blocks = key_piece.reshape(blocks, stripe_rows, local_heads, HD)
     value_blocks = value_piece.reshape(blocks, stripe_rows, local_heads, HD)

time: 312 us -> 313 us (level)
  blocking collectives: 25.6 us -> 13.2 us
  local copies, waits for them, and re-layouts: 11.5 us -> 16.2 us
  waiting for transfers between devices: 227 us -> 231 us
  starting transfers between devices: 2.67 us -> 5.98 us
    all_gather x1 -> x0, blocking collectives: 13 us -> none  [on_device(): value_piece = lax.all_gather(values_image, 'col', axis=0, tiled=True)]
    ppermute x0 -> x3, waiting for transfers between devices: none -> 6.57 us  [on_device(): lax.ppermute(ring[-1], 'col', [(dev, (dev + 1) % 4) for dev in range(4)])]
    unnamed x21 -> x44, local copies, waits for them, and re-layouts: 5.54 us -> 8.99 us
    dot_general x4, matrix products: 4.33 us -> 0.95 us  [one_block(): jnp.einsum('hsk,khd->hsd', weights.astype(jnp.bfloat16), value_block, pre...]
    dot_general x4, matrix products: 1.15 us -> 4.5 us  [one_block(): jnp.einsum('hsd,khd->hsk', queries, key_block, preferred_element_type=jnp...]
  transfers between devices with their start and end apart: 4 -> 7, of which waited for: 4 -> 6; matrix products, arithmetic and copies ran while one was open for 2% -> 4% of each run, Pallas kernels for 0% -> 0%
where the time goes in v1:
time: 313 us
  waiting for transfers between devices  231 us (74%)
  matrix products  18 us (6%)
  local copies, waits for them, and re-layouts  16.2 us (5%)
  between operations  15.5 us (5%)
  blocking collectives  13.2 us (4%)
  other arithmetic  12.2 us (4%)
  starting transfers between devices  5.98 us (2%)
    psum x1, waiting for transfers between devices, on_device(): lax.psum(jnp.dot(attended, output_weight, preferred_element_type=jnp.floa...  125 us
    reduce_scatter x1, waiting for transfers between devices, on_device(): lax.psum_scatter(jnp.dot(hidden, down_weight, preferred_element_type=jnp....  66.2 us
    all_gather x1, waiting for transfers between devices, on_device(): stripe_tokens = lax.all_gather(tokens, 'row', axis=1, tiled=True)  32.3 us
    all_gather x1, blocking collectives, on_device(): key_piece = lax.all_gather(keys_image, 'col', axis=0, tiled=True)  13.2 us
    unnamed x44, local copies, waits for them, and re-layouts  8.99 us
    dot_general x1, matrix products, on_device(): jnp.dot(hidden, down_weight, preferred_element_type=jnp.float32)  7.51 us
    ppermute x3, waiting for transfers between devices, on_device(): lax.ppermute(ring[-1], 'col', [(dev, (dev + 1) % 4) for dev in range(4)])  6.57 us
  transfers between devices with their start and end apart: 7, of which 6 were waited for; matrix products, arithmetic and copies ran while one was open for 4% of the time, Pallas kernels for 0%

profile of v1, /device:TPU:8, one launch (start us, length us, event | category | flops | bytes accessed | tf_op | source)
XLA Modules:
  0.0 312.6 jit_solution(13941066035452799763)
XLA Ops:
  8.0 4.1 %copy.26 = bf16[2432,3,128]{0,2,1:T(8,128)(2,1)} copy(bf16[2432,3,128]{2,0,1:T(8,128)(2,1)} %param.18) | data formatting | bytes 3735552 | tf_op args[4]
  15.9 32.3 %all-gather.2.cloned.1.call-done = bf16[1,16,16,2432]{3,2,0,1:T(8,128)(2,1)} async-done(((bf16[1,1,16,2432]{3,2,0,1:T(8,128)(2,1)}), bf16[1,16,16,2432]{3,2,0,1:T(8,128)(2,1)}) %all-gather.2.cloned.1.call-update) | async-done | bytes 1245200 | tf_op jit(solution)/shard_map/all_gather | solution.py:59
  48.2 1.7 convert_reduce_fusion
  49.9 1.7 multiply_reduce_fusion.1
  53.1 1.6 collective-permute-start
  55.3 2.2 collective-permute-done
  57.5 1.5 collective-permute-start.1
  59.0 13.2 %all_gather.7 = bf16[1024,128]{0,1:T(8,128)(2,1)} all-gather(bf16[256,128]{0,1:T(8,128)(2,1)S(1)} %fusion.35), channel_id=1, replica_groups=mesh['row'=16,'col'=4,'item'=4] {'col'}, dimensions={0}, use_global_device_ids=true | all-gather | bytes 327680 | tf_op jit(solution)/shard_map/all_gather | solution.py:114
  72.2 1.8 reshape.190
  74.0 1.7 copy.29
  75.8 4.4 %collective-permute-done.2 = bf16[256,128]{0,1:T(8,128)(2,1)S(1)} collective-permute-done((bf16[256,128]{0,1:T(8,128)(2,1)}, bf16[256,128]{0,1:T(8,128)(2,1)S(1)}, u32[]{:S(2)}, u32[]{:S(2)}) %collective-permute-start.2) | collective-permute-done | bytes 65568 | tf_op jit(solution)/shard_map/ppermute | solution.py:117
  85.5 6.1 %while.14 = (s32[]{:T(128)}, f32[2,256]{1,0:T(2,128)S(1)}, f32[2,256]{1,0:T(2,128)S(1)}, f32[2,256,64]{1,2,0:T(8,128)S(1)}, bf16[4,256,2,64]{1,3,2,0:T(8,128)(2,...) while((s32[]{:T(128)}, f32[2,256]{1,0:T(2,128)S(1)}, ...), condition=%wide.region_9.10_spmd, body=%wide.region_6.9_spmd.sunk | while | flops 34407424 | bytes 2064985 | solution.py:124
  85.5 1.1 fusion.75
  88.6 1.1 fusion.75
  90.1 1.1 fusion.75
  91.7 2.7 convolution_convert_fusion
  94.4 124.6 %all-reduce.2.cloned.1.call-done = bf16[256,2432]{1,0:T(8,128)(2,1)} async-done(((bf16[256,2432]{1,0:T(8,128)(2,1)}), bf16[256,2432]{1,0:T(8,128)(2,1)}) %all-reduce.2.cloned.1.call-update) | async-done | bytes 1245200 | tf_op jit(solution)/shard_map/psum | solution.py:134
  219.0 2.2 fusion.51
  221.2 1.4 copy-done.2
  223.0 7.5 %convolution_convert_fusion.1 = bf16[256,2432]{1,0:T(8,128)(2,1)} fusion(bf16[608,2432]{1,0:T(8,128)(2,1)S(1)} %copy-done, bf16[2432,608]{0,1:T(8,128)(2,1)} %param.21, f32[256,2432]{1,0:T(8,128)} %copy-done.2, f32[2432]{0:T(1024)S(1)} %copy-done.13, f32[2432]{0:T(1024)S(1)} %copy-done.14, f32[256]{0:T(256)S(1)} %add_rsqrt_fusion.3, ...), kind=kOutput, calls=%fused_computation.16 | convolution fusion | flops 1519280128 | bytes 9671680 | tf_op jit(solution)/shard_map/dot_general | solution.py:145
  230.6 66.2 %reduce-scatter.2.cloned.1.call-done = bf16[16,2432]{1,0:T(8,128)(2,1)} async-done(((bf16[256,2432]{1,0:T(8,128)(2,1)}), bf16[16,2432]{1,0:T(8,128)(2,1)}) %reduce-scatter.2.cloned.1.call-update) | async-done | bytes 77840 | tf_op jit(solution)/shard_map/reduce_scatter | solution.py:144
  297.8 1.7 multiply_reduce_fusion.2
  299.6 1.2 fusion.36
  300.9 2.7 collective-permute-start.3
  (107 shorter events, 17.2 us)
Async XLA Ops:
  7.2 215.8 %copy-start = (bf16[608,2432]{1,0:T(8,128)(2,1)S(1)}, bf16[608,2432]{1,0:T(8,128)(2,1)}, u32[]{:S(2)}) copy-start(bf16[608,2432]{1,0:T(8,128)(2,1)} %param.22) | copy-start | bytes 8871940
  7.2 4.9 %copy-start.4 = (bf16[1,154,2,128]{3,2,1,0:T(2,128)(2,1)S(1)}, bf16[1,154,2,128]{3,2,1,0:T(2,128)(2,1)}, u32[]{:S(2)}) copy-start(bf16[1,154,2,128]{3,2,1,0:T(2,128)(2,1)} %param.15) | copy-start | bytes 236548
  7.2 7.2 %copy-start.16 = (f32[2,64]{1,0:T(2,128)S(1)}, f32[2,64]{1,0:T(2,128)}, u32[]{:S(2)}) copy-start(f32[2,64]{1,0:T(2,128)} %param.19) | copy-start | bytes 1540
  7.2 7.9 %copy-start.9 = (f32[1,8,2432]{2,1,0:T(8,128)S(1)}, f32[1,8,2432]{2,1,0:T(8,128)}, u32[]{:S(2)}) copy-start(f32[1,8,2432]{2,1,0:T(8,128)} %param.17) | copy-start | bytes 233476
  7.2 41.0 %all-gather.2.cloned.1.call-start = ((), (), s32[]{:S(2)}) async-start(), calls=%async_computation.1 | async-start | bytes 1323008 | tf_op jit(solution)/shard_map/all_gather | solution.py:59
  7.9 211.0 %all-reduce.2.cloned.1.call-start = ((), (), s32[]{:S(2)}) async-start(), calls=%async_computation.2 | async-start | bytes 2490368 | tf_op jit(solution)/shard_map/psum | solution.py:134
  48.2 3.5 %copy-start.1 = (bf16[1,16,16,2432]{3,2,0,1:T(8,128)(2,1)S(1)}, bf16[1,16,16,2432]{3,2,0,1:T(8,128)(2,1)}, u32[]{:S(2)}) copy-start(bf16[1,16,16,2432]{3,2,0,1:T(8,128)(2,1)} %all-gather.2.cloned.1.call-done) | copy-start | bytes 3735556
  48.2 4.1 %copy-start.3 = (bf16[2432,3,128]{0,2,1:T(8,128)(2,1)S(1)}, bf16[2432,3,128]{0,2,1:T(8,128)(2,1)}, u32[]{:S(2)}) copy-start(bf16[2432,3,128]{0,2,1:T(8,128)(2,1)} %copy.26) | copy-start | bytes 5603332
  52.2 2.5 copy-start.6
  52.3 2.5 copy-start.17
  52.3 2.8 copy-start.7
  53.1 4.4 %collective-permute-start = (bf16[256,128]{0,1:T(8,128)(2,1)S(1)}, bf16[256,128]{0,1:T(8,128)(2,1)}, u32[]{:S(2)}, u32[]{:S(2)}) collective-permute-start(bf16[256,128]{0,1:T(8,128)(2,1)S(1)} %bitcast.81), channel_id=1, source_target_pairs={{0,4},{4,8},{8,12},{12,0},{1,5},{5,9},{9,13},{13,1},{2,6},{6,10},{... | collective-permute-start | bytes 196616 | tf_op jit(solution)/shard_map/ppermute | solution.py:117
  57.5 18.2 %collective-permute-start.1 = (bf16[256,128]{0,1:T(8,128)(2,1)}, bf16[256,128]{0,1:T(8,128)(2,1)}, u32[]{:S(2)}, u32[]{:S(2)}) collective-permute-start(bf16[256,128]{0,1:T(8,128)(2,1)} %collective-permute-done), channel_id=1, source_target_pairs={{0,4},{4,8},{8,12},{12,0},{1,5},{5,9},{9,13},{13,1},{2,6},{6,10},{... | collective-permute-start | bytes 196616 | tf_op jit(solution)/shard_map/ppermute | solution.py:117
  75.7 4.5 %collective-permute-start.2 = (bf16[256,128]{0,1:T(8,128)(2,1)}, bf16[256,128]{0,1:T(8,128)(2,1)S(1)}, u32[]{:S(2)}, u32[]{:S(2)}) collective-permute-start(bf16[256,128]{0,1:T(8,128)(2,1)} %collective-permute-done.1), channel_id=1, source_target_pairs={{0,4},{4,8},{8,12},{12,0},{1,5},{5,9},{9,13},{13,1},{2,6},{6,10},{... | collective-permute-start | bytes 196616 | tf_op jit(solution)/shard_map/ppermute | solution.py:117
  91.6 127.3 %copy-start.10 = (f32[2432]{0:T(1024)S(1)}, f32[2432]{0:T(1024)}, u32[]{:S(2)}) copy-start(f32[2432]{0:T(1024)} %get-tuple-element.63) | copy-start | bytes 29188
  94.3 202.4 %reduce-scatter.2.cloned.1.call-start = ((), (), s32[]{:S(2)}) async-start(), calls=%async_computation.3 | async-start | bytes 1323008 | tf_op jit(solution)/shard_map/reduce_scatter | solution.py:144
  221.1 1.9 copy-start.13
  221.1 1.9 copy-start.14
  223.0 73.7 %copy-start.8 = (f32[2432]{0:T(1024)S(1)}, f32[2432]{0:T(1024)}, u32[]{:S(2)}) copy-start(f32[2432]{0:T(1024)} %get-tuple-element.60) | copy-start | bytes 29188
  223.0 76.6 %copy-start.5 = (bf16[2432,64]{0,1:T(8,128)(2,1)S(1)}, bf16[2432,64]{0,1:T(8,128)(2,1)}, u32[]{:S(2)}) copy-start(bf16[2432,64]{0,1:T(8,128)(2,1)} %param.23) | copy-start | bytes 933892
  223.0 76.6 %copy-start.11 = (f32[2432]{0:T(1024)S(1)}, f32[2432]{0:T(1024)}, u32[]{:S(2)}) copy-start(f32[2432]{0:T(1024)} %get-tuple-element.57) | copy-start | bytes 29188
  223.0 76.6 %copy-start.12 = (f32[2432]{0:T(1024)S(1)}, f32[2432]{0:T(1024)}, u32[]{:S(2)}) copy-start(f32[2432]{0:T(1024)} %get-tuple-element.64) | copy-start | bytes 29188
  230.6 74.9 %copy-start.15 = (f32[1,1,1024]{2,1,0:T(1,128)S(1)}, f32[1,1,1024]{2,1,0:T(1,128)}, u32[]{:S(2)}) copy-start(f32[1,1,1024]{2,1,0:T(1,128)} %param.25) | copy-start | bytes 12292
  300.9 4.5 %collective-permute-start.3 = (f32[1,1,1024]{2,1,0:T(1,128)S(1)}, f32[1,1,1024]{2,1,0:T(1,128)S(1)}, u32[]{:S(2)}, u32[]{:S(2)}) collective-permute-start(f32[1,1,1024]{2,1,0:T(1,128)S(1)} %reshape.194), channel_id=1, source_target_pairs={{0,1},{1,0},{2,3},{3,2},{4,5},{5,4},{6,7},{7,6},{8,9},{9,8},{10,11... | collective-permute-start | bytes 12296 | tf_op jit(solution)/shard_map/ppermute | solution.py:17
  (1 other events, 1.4 us)
Sparse Core Ops, SparseCore 0:
  9.9 38.2 all-gather.1
  94.5 124.4 all-reduce.1
  230.7 65.9 reduce-scatter.1
